TPU v7x, 512 devices: a whole 4x8x8 slice. The times are simulated.
512 devices in a mesh: replica: 32 (over z, x), tensor: 16 (over y, core).
Axes of the slice: x: 4, y: 8, z: 8, core: 2. Of those that a mesh axis runs over, the one named last changes fastest.
Arguments:
- hidden_acts: bfloat16 [16384, 16384], P('replica', 'tensor'), may hold values from -6 to 6
- out_grad: bfloat16 [16384, 768], P('replica'), may hold values from -0.25 to 0.25
- error_prev: bfloat16 [32, 768, 16384], P('replica', None, 'tensor'), may hold values from -6 to 6
- right_prev: bfloat16 [16384, 128], P('tensor'), may hold values from -6 to 6
Outputs:
- error_next: bfloat16 [32, 768, 16384], P('replica', None, 'tensor')
- right_next: float32 [16384, 128], P('tensor')
All inputs are finite; a program needn't handle non-finite values.
Results may differ from a plain program's by a relative error of at most 0.0058.
Values may be sent and summed in bfloat16 or wider, within the bound.
No kernel may reach another device: no remote copies, remote signals or barrier semaphores. Data moves between devices by JAX's collectives and lax.ppermute only.
A program may use at most 64 MiB of HBM per device.

v0:
```python
import jax
import jax.numpy as jnp
from jax import lax
from jax.sharding import PartitionSpec as P


def split_up(value, dim, count):
    lengths = value.shape
    blocks = value.reshape(*lengths[:dim], count, lengths[dim] // count, *lengths[dim + 1 :])
    return jnp.moveaxis(blocks, dim, 0)


def sum_at_owner(value, axis, dim):
    blocks = split_up(value, dim, lax.axis_size(axis))
    arrived = lax.all_to_all(blocks, axis, split_axis=0, concat_axis=0, tiled=True)
    return arrived.sum(axis=0)


def copy_for_each(value, axis):
    copies = jnp.broadcast_to(value, (lax.axis_size(axis), *value.shape))
    return lax.all_to_all(copies, axis, split_axis=0, concat_axis=0, tiled=True)


def of_everyone(value, axis):
    return copy_for_each(value, axis).sum(axis=0)


def laid_out(blocks, dim):
    blocks = jnp.moveaxis(blocks, 0, dim)
    lengths = blocks.shape
    return blocks.reshape(*lengths[:dim], lengths[dim] * lengths[dim + 1], *lengths[dim + 2 :])


def collect(value, axis, dim):
    return laid_out(copy_for_each(value, axis), dim)


def orthonormal(p_rows, gram_matrix):
    factor = jnp.linalg.cholesky(gram_matrix)
    return jax.scipy.linalg.solve_triangular(factor, p_rows.T, lower=True).T.astype(jnp.bfloat16)


def shards(hidden_acts, out_grad, error_prev, right_prev):
    weight_grad = lax.dot_general(
        out_grad, hidden_acts, (((0,), (0,)), ((), ())), preferred_element_type=jnp.float32
    )
    compensated = (weight_grad + error_prev[0].astype(jnp.float32)).astype(jnp.bfloat16)
    partial_value = jnp.dot(compensated, right_prev, preferred_element_type=jnp.float32)
    row_share = sum_at_owner(partial_value, "tensor", 0)
    row_share = of_everyone(row_share, "replica")
    local_gram = jnp.dot(row_share.T, row_share, precision=lax.Precision.HIGHEST)
    gram_matrix = of_everyone(local_gram, "tensor")
    orth_rows = orthonormal(row_share, gram_matrix)
    left_low = collect(orth_rows, "tensor", 0)
    replicas = lax.axis_size("replica")
    share = sum_at_owner(
        lax.dot_general(
            compensated, left_low, (((0,), (0,)), ((), ())), preferred_element_type=jnp.float32
        ),
        "replica",
        0,
    )
    right_next = collect(share / replicas, "replica", 0)
    right_low = right_next.astype(jnp.bfloat16)
    approx = lax.dot_general(
        left_low, right_low, (((1,), (1,)), ((), ())), preferred_element_type=jnp.float32
    )
    error_next = (compensated.astype(jnp.float32) - approx).astype(jnp.bfloat16)
    return (error_next[None], right_next)


def solution(mesh):
    return jax.shard_map(
        shards,
        mesh=mesh,
        in_specs=(
            P("replica", "tensor"),
            P("replica", None),
            P("replica", None, "tensor"),
            P("tensor", None),
        ),
        out_specs=(P("replica", None, "tensor"), P("tensor", None)),
        check_vma=False,
    )
```

profile of v0, /device:TPU:2, one launch (start us, length us, event | category | flops | bytes accessed | tf_op | source)
XLA Modules:
  0.0 181.9 jit_solution(17470188426861781422)
XLA Ops:
  0.6 0.0 copy-start
  0.6 1.2 copy-done
  1.9 0.0 copy-start.1
  1.9 2.7 %fusion = bf16[768,1024]{1,0:T(8,128)(2,1)S(1)} fusion(bf16[512,768]{1,0:T(8,128)(2,1)} %param.5, bf16[512,1024]{1,0:T(8,128)(2,1)S(1)} %copy-done, bf16[1,768,1024]{2,1,0:T(8,128)(2,1)} %param.6), kind=kOutput, calls=%fused_computation.1 | convolution fusion | flops 807665664 | bytes 4980736 | tf_op jit(solution)/shard_map/dot_general | solution.py:44
  4.6 0.0 copy-done.1
  4.6 0.6 fusion.5
  5.2 20.6 %all_to_all.30 = f32[16,48,128]{2,1,0:T(8,128)S(1)} all-to-all(f32[16,48,128]{2,1,0:T(8,128)S(1)} %bitcast.38), channel_id=1, replica_groups=mesh['replica'=32,'tensor'=16] {'tensor'}, dimensions={0} | all-to-all | bytes 786432 | tf_op jit(solution)/shard_map/all_to_all | solution.py:15
  25.8 0.1 broadcast_in_dim.17
  25.9 36.6 %all_to_all.31 = f32[32,48,128]{2,1,0:T(8,128)S(1)} all-to-all(f32[32,48,128]{2,1,0:T(8,128)S(1)} %broadcast_in_dim.17), channel_id=1, replica_groups=mesh['replica'=32,'tensor'=16] {'replica'}, dimensions={0} | all-to-all | bytes 1572864 | tf_op jit(solution)/shard_map/all_to_all | solution.py:21
  62.5 0.1 reduce_sum.37
  62.5 0.3 fusion.6
  62.8 0.1 broadcast_in_dim.18
  62.9 30.5 %all_to_all.32 = f32[16,128,128]{2,1,0:T(8,128)} all-to-all(f32[16,128,128]{2,1,0:T(8,128)S(1)} %broadcast_in_dim.18), channel_id=1, replica_groups=mesh['replica'=32,'tensor'=16] {'tensor'}, dimensions={0} | all-to-all | bytes 2097152 | tf_op jit(solution)/shard_map/all_to_all | solution.py:21
  93.4 1.3 reduce_sum.38
  94.7 0.1 copy.10
  94.8 11.7 %cholesky.16 = f32[128,128]{1,0:T(8,128)S(1)} custom-call(f32[128,128]{1,0:T(8,128)S(1)} %fusion.4), custom_call_target="Cholesky" | custom-call | tf_op jit(solution)/shard_map/jit(cholesky)/cholesky | solution.py:39
  106.5 0.6 compare_reduce_fusion
  107.2 0.7 fusion.2
  107.9 9.8 %custom-call.7 = f32[1,128,128]{1,2,0:T(8,128)S(1)} custom-call(f32[1,128,128]{2,1,0:T(8,128)S(1)} %fusion.2), custom_call_target="InvertDiagBlocksLowerTriangular" | custom-call | tf_op jit(solution)/shard_map/jit(_solve_triangular)/triangular_solve | solution.py:40
  117.7 0.2 convolution_convert_fusion
  117.9 0.7 broadcast_in_dim.19
  118.6 4.2 %all-to-all-start.3 = ((bf16[16,48,128]{2,1,0:T(8,128)(2,1)}), bf16[16,48,128]{2,1,0:T(8,128)(2,1)S(1)}, u32[]{:S(2)}, u32[]{:S(2)}) async-start(bf16[16,48,128]{2,1,0:T(8,128)(2,1)} %broadcast_in_dim.19), calls=%async_computation.3 | async-start | bytes 393216 | tf_op jit(solution)/shard_map/all_to_all | solution.py:21
  122.8 1.6 copy.11
  124.4 8.5 %all-to-all-done.3 = bf16[16,48,128]{2,1,0:T(8,128)(2,1)S(1)} async-done(((bf16[16,48,128]{2,1,0:T(8,128)(2,1)}), bf16[16,48,128]{2,1,0:T(8,128)(2,1)S(1)}, u32[]{:S(2)}, u32[]{:S(2)}) %all-to-all-start.3) | async-done | bytes 196640 | tf_op jit(solution)/shard_map/all_to_all | solution.py:21
  132.9 2.0 %fusion.7 = f32[32,32,128]{2,1,0:T(8,128)S(1)} fusion(bf16[32,32,768]{2,1,0:T(8,128)(2,1)} %bitcast.34, bf16[768,128,1]{1,0,2:T(8,128)(2,1)S(1)} %bitcast.36), kind=kOutput, calls=%fused_computation.17 | convolution fusion | flops 201326592 | bytes 2293760 | tf_op jit(solution)/shard_map/dot_general | solution.py:57
  134.8 22.8 %all_to_all.33 = f32[32,32,128]{2,1,0:T(8,128)S(1)} all-to-all(f32[32,32,128]{2,1,0:T(8,128)S(1)} %fusion.7), channel_id=1, replica_groups=mesh['replica'=32,'tensor'=16] {'replica'}, dimensions={0} | all-to-all | bytes 1048576 | tf_op jit(solution)/shard_map/all_to_all | solution.py:15
  157.7 0.1 broadcast_in_dim.20
  157.8 21.6 %all_to_all.34 = f32[32,32,128]{2,1,0:T(8,128)S(1)} all-to-all(f32[32,32,128]{2,1,0:T(8,128)S(1)} %broadcast_in_dim.20), channel_id=1, replica_groups=mesh['replica'=32,'tensor'=16] {'replica'}, dimensions={0} | all-to-all | bytes 1048576 | tf_op jit(solution)/shard_map/all_to_all | solution.py:21
  179.4 1.7 fusion.1
  181.1 0.8 copy.13
  (6 shorter events, 0.2 us)
Async XLA Ops:
  0.6 1.2 copy-start
  1.9 2.7 %copy-start.1 = (bf16[1024,128]{1,0:T(8,128)(2,1)S(1)}, bf16[1024,128]{1,0:T(8,128)(2,1)}, u32[]{:S(2)}) copy-start(bf16[1024,128]{1,0:T(8,128)(2,1)} %param.7) | copy-start | bytes 786436
  118.6 14.3 %all-to-all-start.3 = ((bf16[16,48,128]{2,1,0:T(8,128)(2,1)}), bf16[16,48,128]{2,1,0:T(8,128)(2,1)S(1)}, u32[]{:S(2)}, u32[]{:S(2)}) async-start(bf16[16,48,128]{2,1,0:T(8,128)(2,1)} %broadcast_in_dim.19), calls=%async_computation.3 | async-start | bytes 393216 | tf_op jit(solution)/shard_map/all_to_all | solution.py:21
where the time goes:
time: 182 us
  blocking collectives  132 us (73%)
  other arithmetic  24.3 us (13%)
  waiting for transfers between devices  8.5 us (5%)
  matrix products  7.43 us (4%)
  local copies, waits for them, and re-layouts  4.58 us (3%)
  starting transfers between devices  4.22 us (2%)
    all_to_all x3, blocking collectives, copy_for_each(): return lax.all_to_all(copies, axis, split_axis=0, concat_axis=0, tiled=True)  88.6 us
    all_to_all x2, blocking collectives, sum_at_owner(): lax.all_to_all(blocks, axis, split_axis=0, concat_axis=0, tiled=True)  43.4 us
    another operation x3, other arithmetic, orthonormal(): factor = jnp.linalg.cholesky(gram_matrix)  12.4 us
    another operation x2, other arithmetic, orthonormal(): jax.scipy.linalg.solve_triangular(factor, p_rows.T, lower=True)  10.5 us
    all_to_all x1, waiting for transfers between devices, copy_for_each(): return lax.all_to_all(copies, axis, split_axis=0, concat_axis=0, tiled=True)  8.5 us
    all_to_all x1, starting transfers between devices, copy_for_each(): return lax.all_to_all(copies, axis, split_axis=0, concat_axis=0, tiled=True)  4.22 us
  transfers between devices with their start and end apart: 1, of which 1 were waited for; matrix products, arithmetic and copies ran while one was open for 1% of the time, Pallas kernels for 0%

commit v1 on v0

v1 whole, which is shorter than its diff:
```python
import jax
import jax.numpy as jnp
from jax import lax
from jax.experimental import pallas as pl
from jax.experimental.pallas import tpu as pltpu
from jax.sharding import PartitionSpec as P

EXACT = lax.Precision.HIGHEST
SUB, LANE = 8, 128
PIVOTS = 8
PANEL = 64


def sum_at_owner(value, axis):
    parts = lax.axis_size(axis)
    blocks = value.reshape(parts, value.shape[0] // parts, value.shape[1])
    return lax.all_to_all(blocks, axis, split_axis=0, concat_axis=0, tiled=True)


def copy_for_each(value, axis):
    copies = jnp.broadcast_to(value, (lax.axis_size(axis), *value.shape))
    return lax.all_to_all(copies, axis, split_axis=0, concat_axis=0, tiled=True)


def collect(value, axis):
    return copy_for_each(value, axis).reshape(-1, value.shape[1])


def eliminate(gram, right, base):
    height, width = gram.shape
    groups = height // SUB
    gram = gram.reshape(groups, SUB, width)
    right = right.reshape(groups, SUB, width)
    shape = (groups, SUB, width)
    row_index = lax.broadcasted_iota(jnp.int32, shape, 0) * SUB + lax.broadcasted_iota(
        jnp.int32, shape, 1
    )

    def row(value, i):
        return jnp.broadcast_to(value[i // SUB, i % SUB : i % SUB + 1, :], (SUB, width))

    pivots = []
    for first in range(0, height, PIVOTS):
        columns = [
            jnp.broadcast_to(gram[:, :, base + first + k : base + first + k + 1], shape)
            for k in range(PIVOTS)
        ]
        corner = {
            (i, k): row(columns[k], first + i) for k in range(PIVOTS) for i in range(k + 1)
        }
        gram_rows = [row(gram, first + i) for i in range(PIVOTS)]
        right_rows = [row(right, first + i) for i in range(PIVOTS)]
        factors = []
        for i in range(PIVOTS):
            inverse = 1.0 / corner[i, i]
            pivots.append(corner[i, i][:1])
            for k in range(i + 1, PIVOTS):
                ratio = corner[i, k] * inverse
                for j in range(k, PIVOTS):
                    corner[k, j] = corner[k, j] - ratio * corner[i, j]
                columns[k] = columns[k] - columns[i] * ratio
                gram_rows[k] = gram_rows[k] - gram_rows[i] * ratio
                right_rows[k] = right_rows[k] - right_rows[i] * ratio
            factors.append(jnp.where(row_index > first + i, columns[i] * inverse, 0.0))
        for i in range(PIVOTS):
            gram = gram - factors[i] * gram_rows[i]
            right = right - factors[i] * right_rows[i]
    scale = lax.rsqrt(jnp.concatenate(pivots, axis=0))
    return gram.reshape(height, width) * scale, right.reshape(height, width) * scale


def orthonormal_body(p_ref, left_ref):
    p_sum = p_ref[...].astype(jnp.float32)
    gram = lax.dot_general(
        p_sum, p_sum, (((0,), (0,)), ((), ())), precision=EXACT, preferred_element_type=jnp.float32
    )
    rank = gram.shape[0]
    across = lax.broadcasted_iota(jnp.int32, (rank, rank), 0)
    along = lax.broadcasted_iota(jnp.int32, (rank, rank), 1)
    right = jnp.where(across == along, 1.0, 0.0)
    inverse = []
    for base in range(0, rank, PANEL):
        upper, done = eliminate(gram[:PANEL], right[:PANEL], base)
        inverse.append(done)
        if base + PANEL < rank:
            update = lax.dot_general(
                upper,
                jnp.concatenate([upper, done], axis=1),
                (((0,), (0,)), ((), ())),
                precision=EXACT,
                preferred_element_type=jnp.float32,
            )[base + PANEL :]
            gram = gram[PANEL:] - update[:, :rank]
            right = right[PANEL:] - update[:, rank:]
    left_ref[...] = lax.dot_general(
        p_sum,
        jnp.concatenate(inverse, axis=0),
        (((1,), (1,)), ((), ())),
        precision=EXACT,
        preferred_element_type=jnp.float32,
    ).astype(left_ref.dtype)


def orthonormal(p_sum):
    rows, rank = p_sum.shape
    return pl.pallas_call(
        orthonormal_body,
        out_shape=jax.ShapeDtypeStruct((rows, rank), jnp.bfloat16),
        in_specs=[pl.BlockSpec(memory_space=pltpu.VMEM)],
        out_specs=pl.BlockSpec(memory_space=pltpu.VMEM),
        cost_estimate=pl.CostEstimate(
            flops=4 * rows * rank * rank, bytes_accessed=6 * rows * rank, transcendentals=rank
        ),
        name="orthonormal",
    )(p_sum)


def shards(hidden_acts, out_grad, error_prev, right_prev):
    weight_grad = lax.dot_general(
        out_grad, hidden_acts, (((0,), (0,)), ((), ())), preferred_element_type=jnp.float32
    )
    compensated = (weight_grad + error_prev[0].astype(jnp.float32)).astype(jnp.bfloat16)
    partial_value = jnp.dot(compensated, right_prev, preferred_element_type=jnp.float32)
    rows = sum_at_owner(partial_value.astype(jnp.bfloat16), "replica")
    rows = rows.astype(jnp.float32).sum(axis=0)
    rows = copy_for_each(rows, "tensor").sum(axis=0)
    p_sum = collect(rows.astype(jnp.bfloat16), "replica")
    left_low = orthonormal(p_sum)
    share = lax.dot_general(
        compensated, left_low, (((0,), (0,)), ((), ())), preferred_element_type=jnp.float32
    )
    mine = sum_at_owner(share.astype(jnp.bfloat16), "replica").astype(jnp.float32).sum(axis=0)
    mine = mine / lax.axis_size("replica")
    right_low = collect(mine.astype(jnp.bfloat16), "replica")
    approx = lax.dot_general(
        left_low, right_low, (((1,), (1,)), ((), ())), preferred_element_type=jnp.float32
    )
    error_next = (compensated.astype(jnp.float32) - approx).astype(jnp.bfloat16)
    return (error_next[None], right_low.astype(jnp.float32))


def solution(mesh):
    return jax.shard_map(
        shards,
        mesh=mesh,
        in_specs=(
            P("replica", "tensor"),
            P("replica", None),
            P("replica", None, "tensor"),
            P("tensor", None),
        ),
        out_specs=(P("replica", None, "tensor"), P("tensor", None)),
        check_vma=False,
    )
```

time: 182 us -> 106 us (0.58)
  the two profiles are of different devices: /device:TPU:2 before, /device:TPU:64 now
where the time goes in v1:
time: 106 us
  blocking collectives  89.2 us (84%)
  Pallas kernels  7.07 us (7%)
  matrix products  6.61 us (6%)
  local copies, waits for them, and re-layouts  1.31 us (1%)
    all_to_all x3, blocking collectives, copy_for_each(): return lax.all_to_all(copies, axis, split_axis=0, concat_axis=0, tiled=True)  49.1 us
    all_to_all x2, blocking collectives, sum_at_owner(): return lax.all_to_all(blocks, axis, split_axis=0, concat_axis=0, tiled=True)  40.1 us
    pallas_call x1, Pallas kernels, orthonormal(): pl.pallas_call(orthonormal_body, out_shape=jax.ShapeDtypeStruct((rows, ra...  7.07 us
    dot_general x1, matrix products, shards(): lax.dot_general(out_grad, hidden_acts, (((0,), (0,)), ((), ())), preferre...  2.7 us

profile of v1, /device:TPU:64, one launch (start us, length us, event | category | flops | bytes accessed | tf_op | source)
XLA Modules:
  0.0 105.8 jit_solution(547865504218511879)
XLA Ops:
  0.6 0.0 copy-start
  0.6 1.2 %copy-done = bf16[512,1024]{1,0:T(8,128)(2,1)S(1)} copy-done((bf16[512,1024]{1,0:T(8,128)(2,1)S(1)}, bf16[512,1024]{1,0:T(8,128)(2,1)}, u32[]{:S(2)}) %copy-start) | copy-done | bytes 1048600
  1.9 0.0 copy-start.2
  1.9 2.7 %fusion = bf16[768,1024]{1,0:T(8,128)(2,1)S(1)} fusion(bf16[512,768]{1,0:T(8,128)(2,1)} %param.5, bf16[512,1024]{1,0:T(8,128)(2,1)S(1)} %copy-done, bf16[1,768,1024]{2,1,0:T(8,128)(2,1)} %param.6), kind=kOutput, calls=%fused_computation.1 | convolution fusion | flops 807665664 | bytes 4980736 | tf_op jit(solution)/shard_map/dot_general | solution.py:119
  4.6 0.0 copy-done.2
  4.6 0.6 convolution_convert_fusion.1
  5.2 23.2 %all_to_all.25 = bf16[32,24,128]{2,1,0:T(8,128)(2,1)S(1)} all-to-all(bf16[32,24,128]{2,1,0:T(8,128)(2,1)S(1)} %bitcast.21), channel_id=1, replica_groups=mesh['replica'=32,'tensor'=16] {'replica'}, dimensions={0} | all-to-all | bytes 393216 | tf_op jit(solution)/shard_map/all_to_all | solution.py:17
  28.5 16.9 %all_to_all.26 = f32[16,24,128]{2,1,0:T(8,128)S(1)} all-to-all(f32[16,24,128]{2,1,0:T(8,128)S(1)} %broadcast_in_dim.12), channel_id=1, replica_groups=mesh['replica'=32,'tensor'=16] {'tensor'}, dimensions={0} | all-to-all | bytes 393216 | tf_op jit(solution)/shard_map/all_to_all | solution.py:22
  45.4 16.3 %all_to_all.27 = bf16[32,24,128]{2,1,0:T(8,128)(2,1)} all-to-all(bf16[32,24,128]{2,1,0:T(8,128)(2,1)S(1)} %broadcast_in_dim.13), channel_id=1, replica_groups=mesh['replica'=32,'tensor'=16] {'replica'}, dimensions={0} | all-to-all | bytes 393216 | tf_op jit(solution)/shard_map/all_to_all | solution.py:22
  61.7 7.1 %orthonormal.1 = bf16[768,128]{1,0:T(8,128)(2,1)} custom-call(bf16[768,128]{1,0:T(8,128)(2,1)} %bitcast.20), custom_call_target="tpu_custom_call" | custom-call | flops 50331648 | bytes 589824 | tf_op jit(solution)/shard_map/orthonormal/pallas_call | solution.py:106
  68.8 0.0 copy-start.1
  68.8 1.6 %convolution_convert_fusion = bf16[1024,128]{1,0:T(8,128)(2,1)S(1)} fusion(bf16[768,1024]{1,0:T(8,128)(2,1)S(1)} %fusion, bf16[768,128]{1,0:T(8,128)(2,1)} %orthonormal.1), kind=kOutput, calls=%fused_computation.4 | convolution fusion | flops 201457664 | bytes 2031616 | tf_op jit(solution)/shard_map/dot_general | solution.py:129
  70.4 16.8 %all_to_all.28 = bf16[32,32,128]{2,1,0:T(8,128)(2,1)S(1)} all-to-all(bf16[32,32,128]{2,1,0:T(8,128)(2,1)S(1)} %bitcast.19), channel_id=1, replica_groups=mesh['replica'=32,'tensor'=16] {'replica'}, dimensions={0} | all-to-all | bytes 524288 | tf_op jit(solution)/shard_map/all_to_all | solution.py:17
  87.4 15.9 %all_to_all.29 = bf16[32,32,128]{2,1,0:T(8,128)(2,1)S(1)} all-to-all(bf16[32,32,128]{2,1,0:T(8,128)(2,1)S(1)} %broadcast_in_dim.14), channel_id=1, replica_groups=mesh['replica'=32,'tensor'=16] {'replica'}, dimensions={0} | all-to-all | bytes 524288 | tf_op jit(solution)/shard_map/all_to_all | solution.py:22
  103.3 0.0 copy-done.1
  103.3 1.7 %fusion.1 = bf16[1,768,1024]{2,1,0:T(8,128)(2,1)} fusion(bf16[768,128]{1,0:T(8,128)(2,1)S(1)} %copy-done.1, bf16[1024,128]{1,0:T(8,128)(2,1)S(1)} %bitcast.18, bf16[768,1024]{1,0:T(8,128)(2,1)S(1)} %fusion), kind=kOutput, calls=%fused_computation.3 | convolution fusion | flops 203685888 | bytes 3604480 | tf_op jit(solution)/shard_map/dot_general | solution.py:135
  105.0 0.8 bitcast_convert_fusion
  (7 shorter events, 0.2 us)
Async XLA Ops:
  0.6 1.2 %copy-start = (bf16[512,1024]{1,0:T(8,128)(2,1)S(1)}, bf16[512,1024]{1,0:T(8,128)(2,1)}, u32[]{:S(2)}) copy-start(bf16[512,1024]{1,0:T(8,128)(2,1)} %param.4) | copy-start | bytes 3145732
  1.9 2.7 %copy-start.2 = (bf16[1024,128]{1,0:T(8,128)(2,1)S(1)}, bf16[1024,128]{1,0:T(8,128)(2,1)}, u32[]{:S(2)}) copy-start(bf16[1024,128]{1,0:T(8,128)(2,1)} %param.7) | copy-start | bytes 786436
  68.8 34.5 %copy-start.1 = (bf16[768,128]{1,0:T(8,128)(2,1)S(1)}, bf16[768,128]{1,0:T(8,128)(2,1)}, u32[]{:S(2)}) copy-start(bf16[768,128]{1,0:T(8,128)(2,1)} %orthonormal.1) | copy-start | bytes 589828

commit v2 on v1

--- a/solution.py
+++ b/solution.py
@@ -69,10 +69,10 @@
     return gram.reshape(height, width) * scale, right.reshape(height, width) * scale
 
 
-def orthonormal_body(p_ref, left_ref):
-    p_sum = p_ref[...].astype(jnp.float32)
+def factor_body(p_ref, out_ref):
+    p_sum = p_ref[...]
     gram = lax.dot_general(
-        p_sum, p_sum, (((0,), (0,)), ((), ())), precision=EXACT, preferred_element_type=jnp.float32
+        p_sum, p_sum, (((0,), (0,)), ((), ())), preferred_element_type=jnp.float32
     )
     rank = gram.shape[0]
     across = lax.broadcasted_iota(jnp.int32, (rank, rank), 0)
@@ -92,26 +92,29 @@
             )[base + PANEL :]
             gram = gram[PANEL:] - update[:, :rank]
             right = right[PANEL:] - update[:, rank:]
-    left_ref[...] = lax.dot_general(
-        p_sum,
-        jnp.concatenate(inverse, axis=0),
-        (((1,), (1,)), ((), ())),
-        precision=EXACT,
-        preferred_element_type=jnp.float32,
-    ).astype(left_ref.dtype)
+    inverse = jnp.concatenate(inverse, axis=0)
+    high = inverse.astype(jnp.bfloat16)
+    low = (inverse - high.astype(jnp.float32)).astype(jnp.bfloat16)
+    across = (((1,), (1,)), ((), ()))
+    left = lax.dot_general(p_sum, high, across, preferred_element_type=jnp.float32)
+    left = left + lax.dot_general(p_sum, low, across, preferred_element_type=jnp.float32)
+    rows = p_sum.shape[0]
+    out_ref[:rows, :] = left.astype(jnp.bfloat16)
+    out_ref[rows : rows + rank, :] = high
+    out_ref[rows + rank :, :] = low
 
 
-def orthonormal(p_sum):
+def inverse_factor(p_sum):
     rows, rank = p_sum.shape
     return pl.pallas_call(
-        orthonormal_body,
-        out_shape=jax.ShapeDtypeStruct((rows, rank), jnp.bfloat16),
+        factor_body,
+        out_shape=jax.ShapeDtypeStruct((rows + 2 * rank, rank), jnp.bfloat16),
         in_specs=[pl.BlockSpec(memory_space=pltpu.VMEM)],
         out_specs=pl.BlockSpec(memory_space=pltpu.VMEM),
         cost_estimate=pl.CostEstimate(
             flops=4 * rows * rank * rank, bytes_accessed=6 * rows * rank, transcendentals=rank
         ),
-        name="orthonormal",
+        name="inverse_factor",
     )(p_sum)
 
 
@@ -123,14 +126,21 @@
     partial_value = jnp.dot(compensated, right_prev, preferred_element_type=jnp.float32)
     rows = sum_at_owner(partial_value.astype(jnp.bfloat16), "replica")
     rows = rows.astype(jnp.float32).sum(axis=0)
-    rows = copy_for_each(rows, "tensor").sum(axis=0)
+    rows = copy_for_each(rows.astype(jnp.bfloat16), "tensor").astype(jnp.float32).sum(axis=0)
     p_sum = collect(rows.astype(jnp.bfloat16), "replica")
-    left_low = orthonormal(p_sum)
+    rows, rank = p_sum.shape
+    factors = inverse_factor(p_sum)
+    left_low = factors[:rows]
+    inverse = factors[rows : rows + rank].astype(jnp.float32) + factors[rows + rank :].astype(jnp.float32)
+    scaled = inverse / lax.axis_size("replica")
+    left_low, scaled = lax.optimization_barrier((left_low, scaled))
     share = lax.dot_general(
-        compensated, left_low, (((0,), (0,)), ((), ())), preferred_element_type=jnp.float32
+        compensated, p_sum, (((0,), (0,)), ((), ())), preferred_element_type=jnp.float32
     )
     mine = sum_at_owner(share.astype(jnp.bfloat16), "replica").astype(jnp.float32).sum(axis=0)
-    mine = mine / lax.axis_size("replica")
+    mine = lax.dot_general(
+        mine, scaled, (((1,), (1,)), ((), ())), precision=lax.Precision.HIGH, preferred_element_type=jnp.float32
+    )
     right_low = collect(mine.astype(jnp.bfloat16), "replica")
     approx = lax.dot_general(
         left_low, right_low, (((1,), (1,)), ((), ())), preferred_element_type=jnp.float32

time: 106 us -> 97.3 us (0.918)
  the two profiles are of different devices: /device:TPU:64 before, /device:TPU:8 now
where the time goes in v2:
time: 97.3 us; the launch traced here: 96.9 us
  blocking collectives  71.3 us (73%)
  Pallas kernels  6.57 us (7%)
  matrix products  6.45 us (7%)
  waiting for transfers between devices  4.83 us (5%)
  starting transfers between devices  3.87 us (4%)
  other arithmetic  1.78 us (2%)
  local copies, waits for them, and re-layouts  1.38 us (1%)
    all_to_all x3, blocking collectives, copy_for_each(): return lax.all_to_all(copies, axis, split_axis=0, concat_axis=0, tiled=True)  46.7 us
    all_to_all x1, blocking collectives, sum_at_owner(): return lax.all_to_all(blocks, axis, split_axis=0, concat_axis=0, tiled=True)  24.6 us
    pallas_call x1, Pallas kernels, inverse_factor(): pl.pallas_call(factor_body, out_shape=jax.ShapeDtypeStruct((rows + 2 * ra...  6.57 us
    all_to_all x1, waiting for transfers between devices, sum_at_owner(): return lax.all_to_all(blocks, axis, split_axis=0, concat_axis=0, tiled=True)  4.83 us
    all_to_all x1, starting transfers between devices, sum_at_owner(): return lax.all_to_all(blocks, axis, split_axis=0, concat_axis=0, tiled=True)  3.87 us
    dot_general x1, matrix products, shards(): lax.dot_general(out_grad, hidden_acts, (((0,), (0,)), ((), ())), preferre...  2.7 us
  transfers between devices with their start and end apart: 1, of which 1 were waited for; matrix products, arithmetic and copies ran while one was open for 1% of the time, Pallas kernels for 7%

profile of v2, /device:TPU:8, one launch (start us, length us, event | category | flops | bytes accessed | tf_op | source)
XLA Modules:
  0.0 96.9 jit_solution(17479188293593505285)
XLA Ops:
  0.6 0.0 copy-start
  0.6 1.2 %copy-done = bf16[512,1024]{1,0:T(8,128)(2,1)S(1)} copy-done((bf16[512,1024]{1,0:T(8,128)(2,1)S(1)}, bf16[512,1024]{1,0:T(8,128)(2,1)}, u32[]{:S(2)}) %copy-start) | copy-done | bytes 1048600
  1.9 0.0 copy-start.2
  1.9 2.7 %fusion = bf16[768,1024]{1,0:T(8,128)(2,1)S(1)} fusion(bf16[512,768]{1,0:T(8,128)(2,1)} %param.5, bf16[512,1024]{1,0:T(8,128)(2,1)S(1)} %copy-done, bf16[1,768,1024]{2,1,0:T(8,128)(2,1)} %param.6), kind=kOutput, calls=%fused_computation.1 | convolution fusion | flops 807665664 | bytes 4980736 | tf_op jit(solution)/shard_map/dot_general | solution.py:122
  4.6 0.0 copy-done.2
  4.6 0.6 convolution_convert_fusion.1
  5.2 24.6 %all_to_all.25 = bf16[32,24,128]{2,1,0:T(8,128)(2,1)S(1)} all-to-all(bf16[32,24,128]{2,1,0:T(8,128)(2,1)S(1)} %bitcast.23), channel_id=1, replica_groups=mesh['replica'=32,'tensor'=16] {'replica'}, dimensions={0} | all-to-all | bytes 393216 | tf_op jit(solution)/shard_map/all_to_all | solution.py:17
  29.8 14.1 %all_to_all.26 = bf16[16,24,128]{2,1,0:T(8,128)(2,1)S(1)} all-to-all(bf16[16,24,128]{2,1,0:T(8,128)(2,1)S(1)} %broadcast_in_dim.12), channel_id=1, replica_groups=mesh['replica'=32,'tensor'=16] {'tensor'}, dimensions={0} | all-to-all | bytes 196608 | tf_op jit(solution)/shard_map/all_to_all | solution.py:22
  44.0 15.9 %all_to_all.27 = bf16[32,24,128]{2,1,0:T(8,128)(2,1)S(1)} all-to-all(bf16[32,24,128]{2,1,0:T(8,128)(2,1)S(1)} %broadcast_in_dim.13), channel_id=1, replica_groups=mesh['replica'=32,'tensor'=16] {'replica'}, dimensions={0} | all-to-all | bytes 393216 | tf_op jit(solution)/shard_map/all_to_all | solution.py:22
  59.9 0.0 copy-start.1
  59.9 1.3 %convolution_convert_fusion = bf16[1024,128]{1,0:T(8,128)(2,1)} fusion(bf16[768,1024]{1,0:T(8,128)(2,1)S(1)} %fusion, bf16[768,128]{1,0:T(8,128)(2,1)S(1)} %bitcast.21), kind=kOutput, calls=%fused_computation.4 | convolution fusion | flops 201457664 | bytes 2031616 | tf_op jit(solution)/shard_map/dot_general | solution.py:137
  61.3 3.9 %all-to-all-start.3 = ((bf16[32,32,128]{2,1,0:T(8,128)(2,1)}), bf16[32,32,128]{2,1,0:T(8,128)(2,1)S(1)}, u32[]{:S(2)}, u32[]{:S(2)}) async-start(bf16[32,32,128]{2,1,0:T(8,128)(2,1)} %bitcast.3), calls=%async_computation.3 | async-start | bytes 524288 | tf_op jit(solution)/shard_map/all_to_all | solution.py:17
  65.1 0.0 copy-done.1
  65.2 6.6 %inverse_factor.1 = bf16[1024,128]{1,0:T(8,128)(2,1)} custom-call(bf16[768,128]{1,0:T(8,128)(2,1)} %bitcast.22), custom_call_target="tpu_custom_call" | custom-call | flops 50331648 | bytes 589824 | tf_op jit(solution)/shard_map/inverse_factor/pallas_call | solution.py:109
  71.7 0.0 slice-start
  71.7 0.8 add_multiply_fusion
  72.6 4.8 %all-to-all-done.3 = bf16[32,32,128]{2,1,0:T(8,128)(2,1)S(1)} async-done(((bf16[32,32,128]{2,1,0:T(8,128)(2,1)}), bf16[32,32,128]{2,1,0:T(8,128)(2,1)S(1)}, u32[]{:S(2)}, u32[]{:S(2)}) %all-to-all-start.3) | async-done | bytes 262176 | tf_op jit(solution)/shard_map/all_to_all | solution.py:17
  77.4 0.1 convolution_convert_fusion.2
  77.6 0.1 broadcast_in_dim.14
  77.7 16.6 %all_to_all.28 = bf16[32,32,128]{2,1,0:T(8,128)(2,1)S(1)} all-to-all(bf16[32,32,128]{2,1,0:T(8,128)(2,1)S(1)} %broadcast_in_dim.14), channel_id=1, replica_groups=mesh['replica'=32,'tensor'=16] {'replica'}, dimensions={0} | all-to-all | bytes 524288 | tf_op jit(solution)/shard_map/all_to_all | solution.py:22
  94.3 0.0 slice-done
  94.3 1.7 %fusion.1 = bf16[1,768,1024]{2,1,0:T(8,128)(2,1)} fusion(bf16[768,128]{1,0:T(8,128)(2,1)S(1)} %slice-done, bf16[1024,128]{1,0:T(8,128)(2,1)S(1)} %bitcast.20, bf16[768,1024]{1,0:T(8,128)(2,1)S(1)} %fusion), kind=kOutput, calls=%fused_computation.3 | convolution fusion | flops 203685888 | bytes 3604480 | tf_op jit(solution)/shard_map/dot_general | solution.py:145
  96.0 0.8 bitcast_convert_fusion
  (5 shorter events, 0.2 us)
Async XLA Ops:
  0.6 1.2 %copy-start = (bf16[512,1024]{1,0:T(8,128)(2,1)S(1)}, bf16[512,1024]{1,0:T(8,128)(2,1)}, u32[]{:S(2)}) copy-start(bf16[512,1024]{1,0:T(8,128)(2,1)} %param.4) | copy-start | bytes 3145732
  1.9 2.7 %copy-start.2 = (bf16[1024,128]{1,0:T(8,128)(2,1)S(1)}, bf16[1024,128]{1,0:T(8,128)(2,1)}, u32[]{:S(2)}) copy-start(bf16[1024,128]{1,0:T(8,128)(2,1)} %param.7) | copy-start | bytes 786436
  59.9 5.2 %copy-start.1 = (bf16[32,24,128]{2,1,0:T(8,128)(2,1)}, bf16[32,24,128]{2,1,0:T(8,128)(2,1)S(1)}, u32[]{:S(2)}) copy-start(bf16[32,24,128]{2,1,0:T(8,128)(2,1)S(1)} %all_to_all.27) | copy-start | bytes 589828
  61.3 16.1 %all-to-all-start.3 = ((bf16[32,32,128]{2,1,0:T(8,128)(2,1)}), bf16[32,32,128]{2,1,0:T(8,128)(2,1)S(1)}, u32[]{:S(2)}, u32[]{:S(2)}) async-start(bf16[32,32,128]{2,1,0:T(8,128)(2,1)} %bitcast.3), calls=%async_computation.3 | async-start | bytes 524288 | tf_op jit(solution)/shard_map/all_to_all | solution.py:17
  71.7 22.6 %slice-start = ((bf16[1024,128]{1,0:T(8,128)(2,1)}), bf16[768,128]{1,0:T(8,128)(2,1)S(1)}, s32[]{:S(2)}) async-start(bf16[1024,128]{1,0:T(8,128)(2,1)} %inverse_factor.1), calls=%async_computation.5 | async-start | bytes 393216 | tf_op jit(solution)/shard_map/slice | solution.py:133

commit v3 on v2

--- a/solution.py
+++ b/solution.py
@@ -9,6 +9,7 @@
 SUB, LANE = 8, 128
 PIVOTS = 8
 PANEL = 64
+CHUNKS = 4
 
 
 def sum_at_owner(value, axis):
@@ -31,25 +32,25 @@
     groups = height // SUB
     gram = gram.reshape(groups, SUB, width)
     right = right.reshape(groups, SUB, width)
-    shape = (groups, SUB, width)
-    row_index = lax.broadcasted_iota(jnp.int32, shape, 0) * SUB + lax.broadcasted_iota(
-        jnp.int32, shape, 1
-    )
 
     def row(value, i):
         return jnp.broadcast_to(value[i // SUB, i % SUB : i % SUB + 1, :], (SUB, width))
 
     pivots = []
+    finished = []
     for first in range(0, height, PIVOTS):
+        left = (height - first) // SUB
+        shape = (left, SUB, width)
+        row_index = lax.broadcasted_iota(jnp.int32, shape, 0) * SUB + lax.broadcasted_iota(
+            jnp.int32, shape, 1
+        )
         columns = [
             jnp.broadcast_to(gram[:, :, base + first + k : base + first + k + 1], shape)
             for k in range(PIVOTS)
         ]
-        corner = {
-            (i, k): row(columns[k], first + i) for k in range(PIVOTS) for i in range(k + 1)
-        }
-        gram_rows = [row(gram, first + i) for i in range(PIVOTS)]
-        right_rows = [row(right, first + i) for i in range(PIVOTS)]
+        corner = {(i, k): row(columns[k], i) for k in range(PIVOTS) for i in range(k + 1)}
+        gram_rows = [row(gram, i) for i in range(PIVOTS)]
+        right_rows = [row(right, i) for i in range(PIVOTS)]
         factors = []
         for i in range(PIVOTS):
             inverse = 1.0 / corner[i, i]
@@ -61,11 +62,14 @@
                 columns[k] = columns[k] - columns[i] * ratio
                 gram_rows[k] = gram_rows[k] - gram_rows[i] * ratio
                 right_rows[k] = right_rows[k] - right_rows[i] * ratio
-            factors.append(jnp.where(row_index > first + i, columns[i] * inverse, 0.0))
+            factors.append(jnp.where(row_index > i, columns[i] * inverse, 0.0))
         for i in range(PIVOTS):
             gram = gram - factors[i] * gram_rows[i]
             right = right - factors[i] * right_rows[i]
+        finished.append((gram[: PIVOTS // SUB], right[: PIVOTS // SUB]))
+        gram, right = gram[PIVOTS // SUB :], right[PIVOTS // SUB :]
     scale = lax.rsqrt(jnp.concatenate(pivots, axis=0))
+    gram, right = (jnp.concatenate(parts, axis=0) for parts in zip(*finished, strict=True))
     return gram.reshape(height, width) * scale, right.reshape(height, width) * scale
 
 
@@ -114,8 +118,52 @@
         cost_estimate=pl.CostEstimate(
             flops=4 * rows * rank * rank, bytes_accessed=6 * rows * rank, transcendentals=rank
         ),
+        compiler_params=pltpu.CompilerParams(vmem_limit_bytes=8 * 1024 * 1024),
         name="inverse_factor",
     )(p_sum)
+
+
+def outputs_body(left_ref, right_ref, value_ref, error_ref, next_ref, error, wide, done):
+    right = right_ref[...]
+    wide[...] = right.astype(jnp.float32)
+    copies = [pltpu.make_async_copy(wide, next_ref, done.at[CHUNKS])]
+    copies[0].start()
+    rows = value_ref.shape[0] // CHUNKS
+    for i in range(CHUNKS):
+        own = pl.ds(i * rows, rows)
+        approx = lax.dot_general(
+            left_ref[own, :], right, (((1,), (1,)), ((), ())), preferred_element_type=jnp.float32
+        )
+        error[own, :] = (value_ref[own, :].astype(jnp.float32) - approx).astype(error.dtype)
+        copies.append(pltpu.make_async_copy(error.at[own], error_ref.at[0, own], done.at[i]))
+        copies[-1].start()
+    for copy in copies:
+        copy.wait()
+
+
+def outputs(left_low, right_low, compensated):
+    (rows, width), (_, rank) = compensated.shape, right_low.shape
+    return pl.pallas_call(
+        outputs_body,
+        out_shape=(
+            jax.ShapeDtypeStruct((1, rows, width), jnp.bfloat16),
+            jax.ShapeDtypeStruct((width, rank), jnp.float32),
+        ),
+        in_specs=[pl.BlockSpec(memory_space=pltpu.VMEM)] * 3,
+        out_specs=(pl.BlockSpec(memory_space=pl.ANY),) * 2,
+        scratch_shapes=[
+            pltpu.VMEM((rows, width), jnp.bfloat16),
+            pltpu.VMEM((width, rank), jnp.float32),
+            pltpu.SemaphoreType.DMA((CHUNKS + 1,)),
+        ],
+        cost_estimate=pl.CostEstimate(
+            flops=2 * rows * width * rank,
+            bytes_accessed=4 * rows * width + 4 * width * rank,
+            transcendentals=0,
+        ),
+        compiler_params=pltpu.CompilerParams(vmem_limit_bytes=16 * 1024 * 1024),
+        name="outputs",
+    )(left_low, right_low, compensated)
 
 
 def shards(hidden_acts, out_grad, error_prev, right_prev):
@@ -142,11 +190,7 @@
         mine, scaled, (((1,), (1,)), ((), ())), precision=lax.Precision.HIGH, preferred_element_type=jnp.float32
     )
     right_low = collect(mine.astype(jnp.bfloat16), "replica")
-    approx = lax.dot_general(
-        left_low, right_low, (((1,), (1,)), ((), ())), preferred_element_type=jnp.float32
-    )
-    error_next = (compensated.astype(jnp.float32) - approx).astype(jnp.bfloat16)
-    return (error_next[None], right_low.astype(jnp.float32))
+    return outputs(left_low, right_low, compensated)
 
 
 def solution(mesh):

time: 97.3 us -> 95.2 us (0.978)
  waiting for transfers between devices: 4.83 us -> 7.42 us
  matrix products: 6.45 us -> 4.73 us
  other arithmetic: 1.78 us -> 0.13 us
  blocking collectives: 71.3 us -> 70.3 us
    all_to_all x1, waiting for transfers between devices: 4.83 us -> 7.42 us  [sum_at_owner(): return lax.all_to_all(blocks, axis, split_axis=0, concat_axis=0, tiled=True)]
    pallas_call x1, Pallas kernels: 6.57 us -> 4.77 us  [inverse_factor(): pl.pallas_call(factor_body, out_shape=jax.ShapeDtypeStruct((rows + 2 * ra...]
    dot_general x1 -> x0, matrix products: 1.72 us -> none  [shards(): lax.dot_general(left_low, right_low, (((1,), (1,)), ((), ())), preferred_...]
    pallas_call x0 -> x1, Pallas kernels: none -> 1.44 us  [outputs(): pl.pallas_call(outputs_body, out_shape=(jax.ShapeDtypeStruct((1, rows, wi...]
    all_to_all x3, blocking collectives: 46.7 us -> 45.7 us  [copy_for_each(): return lax.all_to_all(copies, axis, split_axis=0, concat_axis=0, tiled=True)]
  transfers between devices with their start and end apart: 1 -> 1, of which waited for: 1 -> 1; matrix products, arithmetic and copies ran while one was open for 1% -> 0% of each run, Pallas kernels for 7% -> 5%
where the time goes in v3:
time: 95.2 us; the launch traced here: 94.8 us
  blocking collectives  70.3 us (74%)
  waiting for transfers between devices  7.42 us (8%)
  Pallas kernels  6.21 us (7%)
  matrix products  4.73 us (5%)
  starting transfers between devices  3.87 us (4%)
  local copies, waits for them, and re-layouts  1.38 us (1%)
    all_to_all x3, blocking collectives, copy_for_each(): return lax.all_to_all(copies, axis, split_axis=0, concat_axis=0, tiled=True)  45.7 us
    all_to_all x1, blocking collectives, sum_at_owner(): return lax.all_to_all(blocks, axis, split_axis=0, concat_axis=0, tiled=True)  24.6 us
    all_to_all x1, waiting for transfers between devices, sum_at_owner(): return lax.all_to_all(blocks, axis, split_axis=0, concat_axis=0, tiled=True)  7.42 us
    pallas_call x1, Pallas kernels, inverse_factor(): pl.pallas_call(factor_body, out_shape=jax.ShapeDtypeStruct((rows + 2 * ra...  4.77 us
    all_to_all x1, starting transfers between devices, sum_at_owner(): return lax.all_to_all(blocks, axis, split_axis=0, concat_axis=0, tiled=True)  3.87 us
    dot_general x1, matrix products, shards(): lax.dot_general(out_grad, hidden_acts, (((0,), (0,)), ((), ())), preferre...  2.7 us
  transfers between devices with their start and end apart: 1, of which 1 were waited for; matrix products, arithmetic and copies ran while one was open for 0% of the time, Pallas kernels for 5%

profile of v3, /device:TPU:8, one launch (start us, length us, event | category | flops | bytes accessed | tf_op | source)
XLA Modules:
  0.0 94.8 jit_solution(5594575945128093488)
XLA Ops:
  0.6 0.0 copy-start
  0.6 1.2 %copy-done = bf16[512,1024]{1,0:T(8,128)(2,1)S(1)} copy-done((bf16[512,1024]{1,0:T(8,128)(2,1)S(1)}, bf16[512,1024]{1,0:T(8,128)(2,1)}, u32[]{:S(2)}) %copy-start) | copy-done | bytes 1048600
  1.9 0.0 copy-start.1
  1.9 2.7 %fusion.value_ref = bf16[768,1024]{1,0:T(8,128)(2,1)S(1)} fusion(bf16[512,768]{1,0:T(8,128)(2,1)} %param.5, bf16[512,1024]{1,0:T(8,128)(2,1)S(1)} %copy-done, bf16[1,768,1024]{2,1,0:T(8,128)(2,1)} %param.6), kind=kOutput, calls=%fused_computation.1 | convolution fusion | flops 807665664 | bytes 4980736 | tf_op jit(solution)/shard_map/dot_general | solution.py:170
  4.6 0.0 copy-done.1
  4.6 0.6 convolution_convert_fusion.1
  5.2 24.6 %all_to_all.25 = bf16[32,24,128]{2,1,0:T(8,128)(2,1)S(1)} all-to-all(bf16[32,24,128]{2,1,0:T(8,128)(2,1)S(1)} %bitcast.18), channel_id=1, replica_groups=mesh['replica'=32,'tensor'=16] {'replica'}, dimensions={0} | all-to-all | bytes 393216 | tf_op jit(solution)/shard_map/all_to_all | solution.py:18
  29.8 14.1 %all_to_all.26 = bf16[16,24,128]{2,1,0:T(8,128)(2,1)S(1)} all-to-all(bf16[16,24,128]{2,1,0:T(8,128)(2,1)S(1)} %broadcast_in_dim.9), channel_id=1, replica_groups=mesh['replica'=32,'tensor'=16] {'tensor'}, dimensions={0} | all-to-all | bytes 196608 | tf_op jit(solution)/shard_map/all_to_all | solution.py:23
  44.0 15.9 %all_to_all.27 = bf16[32,24,128]{2,1,0:T(8,128)(2,1)S(1)} all-to-all(bf16[32,24,128]{2,1,0:T(8,128)(2,1)S(1)} %broadcast_in_dim.10), channel_id=1, replica_groups=mesh['replica'=32,'tensor'=16] {'replica'}, dimensions={0} | all-to-all | bytes 393216 | tf_op jit(solution)/shard_map/all_to_all | solution.py:23
  59.9 1.3 %convolution_convert_fusion = bf16[1024,128]{1,0:T(8,128)(2,1)} fusion(bf16[768,1024]{1,0:T(8,128)(2,1)S(1)} %fusion.value_ref, bf16[768,128]{1,0:T(8,128)(2,1)S(1)} %bitcast.15), kind=kOutput, calls=%fused_computation.2 | convolution fusion | flops 201457664 | bytes 2031616 | tf_op jit(solution)/shard_map/dot_general | solution.py:185
  61.3 3.9 %all-to-all-start.3 = ((bf16[32,32,128]{2,1,0:T(8,128)(2,1)}), bf16[32,32,128]{2,1,0:T(8,128)(2,1)S(1)}, u32[]{:S(2)}, u32[]{:S(2)}) async-start(bf16[32,32,128]{2,1,0:T(8,128)(2,1)} %bitcast.3), calls=%async_computation.3 | async-start | bytes 524288 | tf_op jit(solution)/shard_map/all_to_all | solution.py:18
  65.1 4.8 %inverse_factor.1 = bf16[1024,128]{1,0:T(8,128)(2,1)S(1)} custom-call(bf16[768,128]{1,0:T(8,128)(2,1)S(1)} %bitcast.16), custom_call_target="tpu_custom_call" | custom-call | flops 50331648 | bytes 589824 | tf_op jit(solution)/shard_map/inverse_factor/pallas_call | solution.py:113
  70.0 7.4 %all-to-all-done.3 = bf16[32,32,128]{2,1,0:T(8,128)(2,1)S(1)} async-done(((bf16[32,32,128]{2,1,0:T(8,128)(2,1)}), bf16[32,32,128]{2,1,0:T(8,128)(2,1)S(1)}, u32[]{:S(2)}, u32[]{:S(2)}) %all-to-all-start.3) | async-done | bytes 262176 | tf_op jit(solution)/shard_map/all_to_all | solution.py:18
  77.4 0.1 convolution_convert_fusion.2
  77.6 0.1 broadcast_in_dim.11
  77.7 15.7 %all_to_all.28 = bf16[32,32,128]{2,1,0:T(8,128)(2,1)S(1)} all-to-all(bf16[32,32,128]{2,1,0:T(8,128)(2,1)S(1)} %broadcast_in_dim.11), channel_id=1, replica_groups=mesh['replica'=32,'tensor'=16] {'replica'}, dimensions={0} | all-to-all | bytes 524288 | tf_op jit(solution)/shard_map/all_to_all | solution.py:23
  93.3 1.4 %outputs.1 = (bf16[1,768,1024]{2,1,0:T(8,128)(2,1)}, f32[1024,128]{1,0:T(8,128)}) custom-call(bf16[768,128]{1,0:T(8,128)(2,1)S(1)} %slice.12.left_ref, bf16[1024,128]{1,0:T(8,128)(2,1)S(1)} %bitcast.17, bf16[768,1024]{1,0:T(8,128)(2,1)S(1)} %fusion.value_ref), custom_call_target="tpu_custom_call" | custom-call | flops 201326592 | bytes 3670016 | tf_op jit(solution)/shard_map/outputs/pallas_call | solution.py:146
  (7 shorter events, 0.2 us)
Async XLA Ops:
  0.6 1.2 %copy-start = (bf16[512,1024]{1,0:T(8,128)(2,1)S(1)}, bf16[512,1024]{1,0:T(8,128)(2,1)}, u32[]{:S(2)}) copy-start(bf16[512,1024]{1,0:T(8,128)(2,1)} %param.4) | copy-start | bytes 3145732
  1.9 2.7 %copy-start.1 = (bf16[1024,128]{1,0:T(8,128)(2,1)S(1)}, bf16[1024,128]{1,0:T(8,128)(2,1)}, u32[]{:S(2)}) copy-start(bf16[1024,128]{1,0:T(8,128)(2,1)} %param.7) | copy-start | bytes 786436
  61.3 16.1 %all-to-all-start.3 = ((bf16[32,32,128]{2,1,0:T(8,128)(2,1)}), bf16[32,32,128]{2,1,0:T(8,128)(2,1)S(1)}, u32[]{:S(2)}, u32[]{:S(2)}) async-start(bf16[32,32,128]{2,1,0:T(8,128)(2,1)} %bitcast.3), calls=%async_computation.3 | async-start | bytes 524288 | tf_op jit(solution)/shard_map/all_to_all | solution.py:18

commit v4 on v3

--- a/solution.py
+++ b/solution.py
@@ -10,6 +10,7 @@
 PIVOTS = 8
 PANEL = 64
 CHUNKS = 4
+PIECES = 3
 
 
 def sum_at_owner(value, axis):
@@ -123,6 +124,98 @@
     )(p_sum)
 
 
+def compensate_body(
+    grad_hbm, acts_hbm, error_hbm, right_hbm, value_ref, part_ref, grad, acts, error, right, done
+):
+    rows = value_ref.shape[0] // PIECES
+    pieces = [pl.ds(i * rows, rows) for i in range(PIECES)]
+    grad_copy = pltpu.make_async_copy(grad_hbm, grad, done.at[PIECES])
+    acts_copy = pltpu.make_async_copy(acts_hbm, acts, done.at[PIECES + 1])
+    right_copy = pltpu.make_async_copy(right_hbm, right, done.at[PIECES + 2])
+    error_copies = [
+        pltpu.make_async_copy(error_hbm.at[0, own], error.at[own], done.at[i])
+        for i, own in enumerate(pieces)
+    ]
+    grad_copy.start()
+    acts_copy.start()
+    error_copies[0].start()
+    right_copy.start()
+    for copy in error_copies[1:]:
+        copy.start()
+    grad_copy.wait()
+    acts_copy.wait()
+    for i, own in enumerate(pieces):
+        weight_grad = lax.dot_general(
+            grad[:, own], acts[...], (((0,), (0,)), ((), ())), preferred_element_type=jnp.float32
+        )
+        error_copies[i].wait()
+        value = (weight_grad + error[own, :].astype(jnp.float32)).astype(value_ref.dtype)
+        value_ref[own, :] = value
+        if i == 0:
+            right_copy.wait()
+        part_ref[own, :] = jnp.dot(
+            value, right[...], preferred_element_type=jnp.float32
+        ).astype(part_ref.dtype)
+
+
+def compensate(hidden_acts, out_grad, error_prev, right_prev):
+    (tokens, rows), width, rank = out_grad.shape, hidden_acts.shape[1], right_prev.shape[1]
+    values = (out_grad, hidden_acts, error_prev, right_prev)
+    return pl.pallas_call(
+        compensate_body,
+        out_shape=(
+            jax.ShapeDtypeStruct((rows, width), jnp.bfloat16),
+            jax.ShapeDtypeStruct((rows, rank), jnp.bfloat16),
+        ),
+        in_specs=[pl.BlockSpec(memory_space=pl.ANY)] * 4,
+        out_specs=(pl.BlockSpec(memory_space=pltpu.VMEM),) * 2,
+        scratch_shapes=[
+            pltpu.VMEM((tokens, rows), jnp.bfloat16),
+            pltpu.VMEM((tokens, width), jnp.bfloat16),
+            pltpu.VMEM((rows, width), jnp.bfloat16),
+            pltpu.VMEM((width, rank), jnp.bfloat16),
+            pltpu.SemaphoreType.DMA((PIECES + 3,)),
+        ],
+        compiler_params=pltpu.CompilerParams(vmem_limit_bytes=16 * 1024 * 1024),
+        name="compensate",
+    )(*(pltpu.with_memory_space_constraint(value, pltpu.HBM) for value in values))
+
+
+def product_body(value_ref, p_ref, share_ref, share, done):
+    p_rows = p_ref[...].T
+    width = value_ref.shape[1] // CHUNKS
+    copies = []
+    for i in range(CHUNKS):
+        own = pl.ds(i * width, width)
+        part = jnp.dot(p_rows, value_ref[:, own], preferred_element_type=jnp.float32)
+        share[own, :] = part.T.astype(share.dtype)
+        copies.append(pltpu.make_async_copy(share.at[own], share_ref.at[own], done.at[i]))
+        copies[-1].start()
+    for copy in copies:
+        copy.wait()
+
+
+def product(compensated, p_sum):
+    (rows, width), (_, rank) = compensated.shape, p_sum.shape
+    return pl.pallas_call(
+        product_body,
+        out_shape=jax.ShapeDtypeStruct((width, rank), jnp.bfloat16),
+        in_specs=[pl.BlockSpec(memory_space=pltpu.VMEM)] * 2,
+        out_specs=pl.BlockSpec(memory_space=pl.ANY),
+        scratch_shapes=[
+            pltpu.VMEM((width, rank), jnp.bfloat16),
+            pltpu.SemaphoreType.DMA((CHUNKS,)),
+        ],
+        cost_estimate=pl.CostEstimate(
+            flops=2 * rows * width * rank,
+            bytes_accessed=2 * (rows * width + rows * rank + width * rank),
+            transcendentals=0,
+        ),
+        compiler_params=pltpu.CompilerParams(vmem_limit_bytes=16 * 1024 * 1024),
+        name="product",
+    )(compensated, p_sum)
+
+
 def outputs_body(left_ref, right_ref, value_ref, error_ref, next_ref, error, wide, done):
     right = right_ref[...]
     wide[...] = right.astype(jnp.float32)
@@ -167,12 +260,8 @@
 
 
 def shards(hidden_acts, out_grad, error_prev, right_prev):
-    weight_grad = lax.dot_general(
-        out_grad, hidden_acts, (((0,), (0,)), ((), ())), preferred_element_type=jnp.float32
-    )
-    compensated = (weight_grad + error_prev[0].astype(jnp.float32)).astype(jnp.bfloat16)
-    partial_value = jnp.dot(compensated, right_prev, preferred_element_type=jnp.float32)
-    rows = sum_at_owner(partial_value.astype(jnp.bfloat16), "replica")
+    compensated, partial_value = compensate(hidden_acts, out_grad, error_prev, right_prev)
+    rows = sum_at_owner(partial_value, "replica")
     rows = rows.astype(jnp.float32).sum(axis=0)
     rows = copy_for_each(rows.astype(jnp.bfloat16), "tensor").astype(jnp.float32).sum(axis=0)
     p_sum = collect(rows.astype(jnp.bfloat16), "replica")
@@ -182,10 +271,8 @@
     inverse = factors[rows : rows + rank].astype(jnp.float32) + factors[rows + rank :].astype(jnp.float32)
     scaled = inverse / lax.axis_size("replica")
     left_low, scaled = lax.optimization_barrier((left_low, scaled))
-    share = lax.dot_general(
-        compensated, p_sum, (((0,), (0,)), ((), ())), preferred_element_type=jnp.float32
-    )
-    mine = sum_at_owner(share.astype(jnp.bfloat16), "replica").astype(jnp.float32).sum(axis=0)
+    share = product(compensated, p_sum)
+    mine = sum_at_owner(share, "replica").astype(jnp.float32).sum(axis=0)
     mine = lax.dot_general(
         mine, scaled, (((1,), (1,)), ((), ())), precision=lax.Precision.HIGH, preferred_element_type=jnp.float32
     )

time: 95.2 us -> 94.1 us (0.988)
  Pallas kernels: 6.21 us -> 11.1 us
  matrix products: 4.73 us -> 0.13 us
  local copies, waits for them, and re-layouts: 1.38 us -> 0.16 us
    pallas_call x0 -> x2, Pallas kernels: none -> 4.86 us  [the longest x1 3.7 us: compensate(): pl.pallas_call(compensate_body, out_shape=(jax.ShapeDtypeStruct((rows, wi...]
    dot_general x3 -> x0, matrix products: 4.61 us -> none  [the longest x1 2.7 us: shards(): lax.dot_general(out_grad, hidden_acts, (((0,), (0,)), ((), ())), preferre...]
    unnamed x4 -> x0, local copies, waits for them, and re-layouts: 1.23 us -> none
where the time goes in v4:
time: 94.1 us; the launch traced here: 93.8 us
  blocking collectives  70.3 us (75%)
  Pallas kernels  11.1 us (12%)
  waiting for transfers between devices  7.42 us (8%)
  starting transfers between devices  3.88 us (4%)
    all_to_all x3, blocking collectives, copy_for_each(): return lax.all_to_all(copies, axis, split_axis=0, concat_axis=0, tiled=True)  45.7 us
    all_to_all x1, blocking collectives, sum_at_owner(): return lax.all_to_all(blocks, axis, split_axis=0, concat_axis=0, tiled=True)  24.6 us
    all_to_all x1, waiting for transfers between devices, sum_at_owner(): return lax.all_to_all(blocks, axis, split_axis=0, concat_axis=0, tiled=True)  7.42 us
    pallas_call x1, Pallas kernels, inverse_factor(): pl.pallas_call(factor_body, out_shape=jax.ShapeDtypeStruct((rows + 2 * ra...  4.77 us
    all_to_all x1, starting transfers between devices, sum_at_owner(): return lax.all_to_all(blocks, axis, split_axis=0, concat_axis=0, tiled=True)  3.88 us
    pallas_call x1, Pallas kernels, compensate(): pl.pallas_call(compensate_body, out_shape=(jax.ShapeDtypeStruct((rows, wi...  3.7 us
  transfers between devices with their start and end apart: 1, of which 1 were waited for; matrix products, arithmetic and copies ran while one was open for 0% of the time, Pallas kernels for 5%

profile of v4, /device:TPU:8, one launch (start us, length us, event | category | flops | bytes accessed | tf_op | source)
XLA Modules:
  0.0 93.8 jit_solution(519183246547070148)
XLA Ops:
  0.6 3.7 %compensate.1 = (bf16[768,1024]{1,0:T(8,128)(2,1)S(1)}, bf16[768,128]{1,0:T(8,128)(2,1)S(1)}) custom-call(bf16[512,768]{1,0:T(8,128)(2,1)} %grad_hbm.1, bf16[512,1024]{1,0:T(8,128)(2,1)} %acts_hbm.1, bf16[1,768,1024]{2,1,0:T(8,128)(2,1)} %error_hbm.1, bf16[1024,128]{1,0:T(8,128)(2,1)} %right_hbm.1), custom_call_target="tpu_custom_call" | custom-call | tf_op jit(solution)/shard_map/compensate/pallas_call | solution.py:164
  4.3 24.6 %all_to_all.25 = bf16[32,24,128]{2,1,0:T(8,128)(2,1)S(1)} all-to-all(bf16[32,24,128]{2,1,0:T(8,128)(2,1)S(1)} %bitcast.9), channel_id=1, replica_groups=mesh['replica'=32,'tensor'=16] {'replica'}, dimensions={0} | all-to-all | bytes 393216 | tf_op jit(solution)/shard_map/all_to_all | solution.py:19
  29.0 14.1 %all_to_all.26 = bf16[16,24,128]{2,1,0:T(8,128)(2,1)S(1)} all-to-all(bf16[16,24,128]{2,1,0:T(8,128)(2,1)S(1)} %broadcast_in_dim.9), channel_id=1, replica_groups=mesh['replica'=32,'tensor'=16] {'tensor'}, dimensions={0} | all-to-all | bytes 196608 | tf_op jit(solution)/shard_map/all_to_all | solution.py:24
  43.2 15.9 %all_to_all.27 = bf16[32,24,128]{2,1,0:T(8,128)(2,1)S(1)} all-to-all(bf16[32,24,128]{2,1,0:T(8,128)(2,1)S(1)} %broadcast_in_dim.10), channel_id=1, replica_groups=mesh['replica'=32,'tensor'=16] {'replica'}, dimensions={0} | all-to-all | bytes 393216 | tf_op jit(solution)/shard_map/all_to_all | solution.py:24
  59.1 1.2 %product.1 = bf16[1024,128]{1,0:T(8,128)(2,1)} custom-call(bf16[768,1024]{1,0:T(8,128)(2,1)S(1)} %get-tuple-element.8.value_ref, bf16[768,128]{1,0:T(8,128)(2,1)S(1)} %bitcast.6), custom_call_target="tpu_custom_call" | custom-call | flops 201326592 | bytes 2031616 | tf_op jit(solution)/shard_map/product/pallas_call | solution.py:200
  60.3 3.9 %all-to-all-start.3 = ((bf16[32,32,128]{2,1,0:T(8,128)(2,1)}), bf16[32,32,128]{2,1,0:T(8,128)(2,1)S(1)}, u32[]{:S(2)}, u32[]{:S(2)}) async-start(bf16[32,32,128]{2,1,0:T(8,128)(2,1)} %bitcast.2), calls=%async_computation.3 | async-start | bytes 524288 | tf_op jit(solution)/shard_map/all_to_all | solution.py:19
  64.2 4.8 %inverse_factor.1 = bf16[1024,128]{1,0:T(8,128)(2,1)S(1)} custom-call(bf16[768,128]{1,0:T(8,128)(2,1)S(1)} %bitcast.7), custom_call_target="tpu_custom_call" | custom-call | flops 50331648 | bytes 589824 | tf_op jit(solution)/shard_map/inverse_factor/pallas_call | solution.py:114
  69.0 7.4 %all-to-all-done.3 = bf16[32,32,128]{2,1,0:T(8,128)(2,1)S(1)} async-done(((bf16[32,32,128]{2,1,0:T(8,128)(2,1)}), bf16[32,32,128]{2,1,0:T(8,128)(2,1)S(1)}, u32[]{:S(2)}, u32[]{:S(2)}) %all-to-all-start.3) | async-done | bytes 262176 | tf_op jit(solution)/shard_map/all_to_all | solution.py:19
  76.5 0.1 convolution_convert_fusion
  76.6 0.1 broadcast_in_dim.11
  76.7 15.7 %all_to_all.28 = bf16[32,32,128]{2,1,0:T(8,128)(2,1)S(1)} all-to-all(bf16[32,32,128]{2,1,0:T(8,128)(2,1)S(1)} %broadcast_in_dim.11), channel_id=1, replica_groups=mesh['replica'=32,'tensor'=16] {'replica'}, dimensions={0} | all-to-all | bytes 524288 | tf_op jit(solution)/shard_map/all_to_all | solution.py:24
  92.4 1.4 %outputs.1 = (bf16[1,768,1024]{2,1,0:T(8,128)(2,1)}, f32[1024,128]{1,0:T(8,128)}) custom-call(bf16[768,128]{1,0:T(8,128)(2,1)S(1)} %slice.12.left_ref, bf16[1024,128]{1,0:T(8,128)(2,1)S(1)} %bitcast.8, bf16[768,1024]{1,0:T(8,128)(2,1)S(1)} %get-tuple-element.8.value_ref), custom_call_target="tpu_custom_call" | custom-call | flops 201326592 | bytes 3670016 | tf_op jit(solution)/shard_map/outputs/pallas_call | solution.py:239
  (7 shorter events, 0.2 us)
Async XLA Ops:
  60.3 16.1 %all-to-all-start.3 = ((bf16[32,32,128]{2,1,0:T(8,128)(2,1)}), bf16[32,32,128]{2,1,0:T(8,128)(2,1)S(1)}, u32[]{:S(2)}, u32[]{:S(2)}) async-start(bf16[32,32,128]{2,1,0:T(8,128)(2,1)} %bitcast.2), calls=%async_computation.3 | async-start | bytes 524288 | tf_op jit(solution)/shard_map/all_to_all | solution.py:19

commit v5 on v4

--- a/solution.py
+++ b/solution.py
@@ -129,25 +129,39 @@
 ):
     rows = value_ref.shape[0] // PIECES
     pieces = [pl.ds(i * rows, rows) for i in range(PIECES)]
-    grad_copy = pltpu.make_async_copy(grad_hbm, grad, done.at[PIECES])
-    acts_copy = pltpu.make_async_copy(acts_hbm, acts, done.at[PIECES + 1])
-    right_copy = pltpu.make_async_copy(right_hbm, right, done.at[PIECES + 2])
+    half = acts.shape[0] // 2
+    halves = [pl.ds(0, half), pl.ds(half, half)]
+    factor_copies = [
+        [
+            pltpu.make_async_copy(source.at[own], target.at[own], done.at[PIECES + 1 + 2 * i + j])
+            for j, (source, target) in enumerate(((grad_hbm, grad), (acts_hbm, acts)))
+        ]
+        for i, own in enumerate(halves)
+    ]
+    right_copy = pltpu.make_async_copy(right_hbm, right, done.at[PIECES])
     error_copies = [
         pltpu.make_async_copy(error_hbm.at[0, own], error.at[own], done.at[i])
         for i, own in enumerate(pieces)
     ]
-    grad_copy.start()
-    acts_copy.start()
+    for copies in factor_copies:
+        for copy in copies:
+            copy.start()
     error_copies[0].start()
     right_copy.start()
     for copy in error_copies[1:]:
         copy.start()
-    grad_copy.wait()
-    acts_copy.wait()
     for i, own in enumerate(pieces):
-        weight_grad = lax.dot_general(
-            grad[:, own], acts[...], (((0,), (0,)), ((), ())), preferred_element_type=jnp.float32
-        )
+        weight_grad = 0.0
+        for copies, tokens in zip(factor_copies, halves, strict=True):
+            if i == 0:
+                for copy in copies:
+                    copy.wait()
+            weight_grad += lax.dot_general(
+                grad[tokens, own],
+                acts[tokens, :],
+                (((0,), (0,)), ((), ())),
+                preferred_element_type=jnp.float32,
+            )
         error_copies[i].wait()
         value = (weight_grad + error[own, :].astype(jnp.float32)).astype(value_ref.dtype)
         value_ref[own, :] = value
@@ -174,7 +188,7 @@
             pltpu.VMEM((tokens, width), jnp.bfloat16),
             pltpu.VMEM((rows, width), jnp.bfloat16),
             pltpu.VMEM((width, rank), jnp.bfloat16),
-            pltpu.SemaphoreType.DMA((PIECES + 3,)),
+            pltpu.SemaphoreType.DMA((PIECES + 5,)),
         ],
         compiler_params=pltpu.CompilerParams(vmem_limit_bytes=16 * 1024 * 1024),
         name="compensate",

time: 94.1 us -> 93.9 us (level)
  no operation moved by 1% of the time
where the time goes in v5:
time: 93.9 us; the launch traced here: 93.6 us
  blocking collectives  70.3 us (75%)
  Pallas kernels  10.9 us (12%)
  waiting for transfers between devices  7.42 us (8%)
  starting transfers between devices  3.88 us (4%)
    all_to_all x3, blocking collectives, copy_for_each(): return lax.all_to_all(copies, axis, split_axis=0, concat_axis=0, tiled=True)  45.7 us
    all_to_all x1, blocking collectives, sum_at_owner(): return lax.all_to_all(blocks, axis, split_axis=0, concat_axis=0, tiled=True)  24.6 us
    all_to_all x1, waiting for transfers between devices, sum_at_owner(): return lax.all_to_all(blocks, axis, split_axis=0, concat_axis=0, tiled=True)  7.42 us
    pallas_call x1, Pallas kernels, inverse_factor(): pl.pallas_call(factor_body, out_shape=jax.ShapeDtypeStruct((rows + 2 * ra...  4.77 us
    all_to_all x1, starting transfers between devices, sum_at_owner(): return lax.all_to_all(blocks, axis, split_axis=0, concat_axis=0, tiled=True)  3.88 us
    pallas_call x1, Pallas kernels, compensate(): pl.pallas_call(compensate_body, out_shape=(jax.ShapeDtypeStruct((rows, wi...  3.51 us
  transfers between devices with their start and end apart: 1, of which 1 were waited for; matrix products, arithmetic and copies ran while one was open for 0% of the time, Pallas kernels for 5%

profile of v5, /device:TPU:8, one launch (start us, length us, event | category | flops | bytes accessed | tf_op | source)
XLA Modules:
  0.0 93.6 jit_solution(9191332307769891537)
XLA Ops:
  0.6 3.5 %compensate.1 = (bf16[768,1024]{1,0:T(8,128)(2,1)S(1)}, bf16[768,128]{1,0:T(8,128)(2,1)S(1)}) custom-call(bf16[512,768]{1,0:T(8,128)(2,1)} %grad_hbm.1, bf16[512,1024]{1,0:T(8,128)(2,1)} %acts_hbm.1, bf16[1,768,1024]{2,1,0:T(8,128)(2,1)} %error_hbm.1, bf16[1024,128]{1,0:T(8,128)(2,1)} %right_hbm.1), custom_call_target="tpu_custom_call" | custom-call | tf_op jit(solution)/shard_map/compensate/pallas_call | solution.py:178
  4.2 24.6 %all_to_all.25 = bf16[32,24,128]{2,1,0:T(8,128)(2,1)S(1)} all-to-all(bf16[32,24,128]{2,1,0:T(8,128)(2,1)S(1)} %bitcast.9), channel_id=1, replica_groups=mesh['replica'=32,'tensor'=16] {'replica'}, dimensions={0} | all-to-all | bytes 393216 | tf_op jit(solution)/shard_map/all_to_all | solution.py:19
  28.8 14.1 %all_to_all.26 = bf16[16,24,128]{2,1,0:T(8,128)(2,1)S(1)} all-to-all(bf16[16,24,128]{2,1,0:T(8,128)(2,1)S(1)} %broadcast_in_dim.9), channel_id=1, replica_groups=mesh['replica'=32,'tensor'=16] {'tensor'}, dimensions={0} | all-to-all | bytes 196608 | tf_op jit(solution)/shard_map/all_to_all | solution.py:24
  43.0 15.9 %all_to_all.27 = bf16[32,24,128]{2,1,0:T(8,128)(2,1)S(1)} all-to-all(bf16[32,24,128]{2,1,0:T(8,128)(2,1)S(1)} %broadcast_in_dim.10), channel_id=1, replica_groups=mesh['replica'=32,'tensor'=16] {'replica'}, dimensions={0} | all-to-all | bytes 393216 | tf_op jit(solution)/shard_map/all_to_all | solution.py:24
  58.9 1.2 %product.1 = bf16[1024,128]{1,0:T(8,128)(2,1)} custom-call(bf16[768,1024]{1,0:T(8,128)(2,1)S(1)} %get-tuple-element.8.value_ref, bf16[768,128]{1,0:T(8,128)(2,1)S(1)} %bitcast.6), custom_call_target="tpu_custom_call" | custom-call | flops 201326592 | bytes 2031616 | tf_op jit(solution)/shard_map/product/pallas_call | solution.py:214
  60.1 3.9 %all-to-all-start.3 = ((bf16[32,32,128]{2,1,0:T(8,128)(2,1)}), bf16[32,32,128]{2,1,0:T(8,128)(2,1)S(1)}, u32[]{:S(2)}, u32[]{:S(2)}) async-start(bf16[32,32,128]{2,1,0:T(8,128)(2,1)} %bitcast.2), calls=%async_computation.3 | async-start | bytes 524288 | tf_op jit(solution)/shard_map/all_to_all | solution.py:19
  64.0 4.8 %inverse_factor.1 = bf16[1024,128]{1,0:T(8,128)(2,1)S(1)} custom-call(bf16[768,128]{1,0:T(8,128)(2,1)S(1)} %bitcast.7), custom_call_target="tpu_custom_call" | custom-call | flops 50331648 | bytes 589824 | tf_op jit(solution)/shard_map/inverse_factor/pallas_call | solution.py:114
  68.8 7.4 %all-to-all-done.3 = bf16[32,32,128]{2,1,0:T(8,128)(2,1)S(1)} async-done(((bf16[32,32,128]{2,1,0:T(8,128)(2,1)}), bf16[32,32,128]{2,1,0:T(8,128)(2,1)S(1)}, u32[]{:S(2)}, u32[]{:S(2)}) %all-to-all-start.3) | async-done | bytes 262176 | tf_op jit(solution)/shard_map/all_to_all | solution.py:19
  76.3 0.1 convolution_convert_fusion
  76.4 0.1 broadcast_in_dim.11
  76.5 15.7 %all_to_all.28 = bf16[32,32,128]{2,1,0:T(8,128)(2,1)S(1)} all-to-all(bf16[32,32,128]{2,1,0:T(8,128)(2,1)S(1)} %broadcast_in_dim.11), channel_id=1, replica_groups=mesh['replica'=32,'tensor'=16] {'replica'}, dimensions={0} | all-to-all | bytes 524288 | tf_op jit(solution)/shard_map/all_to_all | solution.py:24
  92.2 1.4 %outputs.1 = (bf16[1,768,1024]{2,1,0:T(8,128)(2,1)}, f32[1024,128]{1,0:T(8,128)}) custom-call(bf16[768,128]{1,0:T(8,128)(2,1)S(1)} %slice.12.left_ref, bf16[1024,128]{1,0:T(8,128)(2,1)S(1)} %bitcast.8, bf16[768,1024]{1,0:T(8,128)(2,1)S(1)} %get-tuple-element.8.value_ref), custom_call_target="tpu_custom_call" | custom-call | flops 201326592 | bytes 3670016 | tf_op jit(solution)/shard_map/outputs/pallas_call | solution.py:253
  (7 shorter events, 0.2 us)
Async XLA Ops:
  60.1 16.1 %all-to-all-start.3 = ((bf16[32,32,128]{2,1,0:T(8,128)(2,1)}), bf16[32,32,128]{2,1,0:T(8,128)(2,1)S(1)}, u32[]{:S(2)}, u32[]{:S(2)}) async-start(bf16[32,32,128]{2,1,0:T(8,128)(2,1)} %bitcast.2), calls=%async_computation.3 | async-start | bytes 524288 | tf_op jit(solution)/shard_map/all_to_all | solution.py:19
